TPU v7x, 32 devices: a whole 2x2x4 slice. The times are simulated.
32 devices in a mesh: gx: 4 (over z), gy: 2 (over x), gz: 4 (over y, core).
Axes of the slice: x: 2, y: 2, z: 4, core: 2. Of those that a mesh axis runs over, the one named last changes fastest.
Arguments:
- weights: bfloat16 [32, 32, 32, 2, 8, 512], P('gx', 'gy', 'gz'), may hold values from -6 to 6
- angles: float32 [3, 32, 32, 32, 512], P(None, 'gx', 'gy', 'gz'), may hold values from -3.140625 to 3.140625
- translation: bfloat16 [8, 512, 512], replicated, may hold values from -0.09375 to 0.09375
Outputs:
- transformed: bfloat16 [32, 32, 32, 2, 8, 512], P('gx', 'gy', 'gz')
All inputs are finite; a program needn't handle non-finite values.
Results may differ from a plain program's by a relative error of at most 0.025.
Values may be sent and summed in bfloat16 or wider, within the bound.
A program may use at most 128 MiB of HBM per device.

v0:
```python
import jax
import jax.numpy as jnp
from jax import lax
from jax.experimental import pallas as pl
from jax.experimental.pallas import tpu as pltpu
from jax.sharding import PartitionSpec as P

LEVELS = 3
AXES = ("gx", "gy", "gz")


def sincos(angle):
    half = angle * 0.5
    sq = half * half
    sin_half = -1.0 / 39916800.0
    for c in (1.0 / 362880.0, -1.0 / 5040.0, 1.0 / 120.0, -1.0 / 6.0, 1.0):
        sin_half = sin_half * sq + c
    sin_half = sin_half * half
    cos_half = 1.0 / 479001600.0
    for c in (-1.0 / 3628800.0, 1.0 / 40320.0, -1.0 / 720.0, 1.0 / 24.0, -0.5, 1.0):
        cos_half = cos_half * sq + c
    return 1.0 - 2.0 * sin_half * sin_half, 2.0 * sin_half * cos_half


def halve_sum(terms, axis_name, dim):
    count = lax.axis_size(axis_name)
    bit = lax.axis_index(axis_name) // (count // 2)
    mine = lax.dynamic_index_in_dim(terms, bit, dim, keepdims=True)
    theirs = lax.dynamic_index_in_dim(terms, 1 - bit, dim, keepdims=True)
    pairs = [(i, (i + count // 2) % count) for i in range(count)]
    got = lax.ppermute(theirs, axis_name, pairs)
    return (mine.astype(jnp.float32) + got.astype(jnp.float32)).astype(jnp.bfloat16)


def exchange_low(terms, axis_name, dim):
    count = lax.axis_size(axis_name)
    low = count // 2
    if low == 1:
        return terms
    groups = [[h * low + i for i in range(low)] for h in range(2)]
    return lax.all_to_all(
        terms, axis_name, split_axis=dim, concat_axis=dim, axis_index_groups=groups, tiled=True
    )


def rotate_sum(current, angle):
    cosine, sine = sincos(angle.astype(jnp.float32))
    cosine = cosine[..., None, :]
    sine = sine[..., None, :]
    re = current[0].astype(jnp.float32)
    im = current[1].astype(jnp.float32)
    return re * cosine - im * sine, re * sine + im * cosine


def shards(weights, angles, translation):
    counts = [lax.axis_size(a) for a in AXES]
    count_x, count_y, count_z = counts
    devices = count_x * count_y * count_z
    count_yz = count_y * count_z
    top = 2**LEVELS
    hx, hy, hz = (top // c for c in counts)
    lx, ly, lz = (weights.shape[0] // hx, weights.shape[1] // hy, weights.shape[2] // hz)
    rhs, cheb = weights.shape[4], weights.shape[5]
    blocks = lx * ly * lz
    share = blocks * rhs // devices
    block_share = max(1, blocks // devices)
    rhs_share = share // block_share
    repeat = max(1, devices // blocks)
    C = hx * hy * hz

    ph = angles[1:].astype(jnp.bfloat16)
    ph = ph.reshape(LEVELS - 1, hx, lx, hy, ly, hz, lz, cheb).transpose(1, 3, 5, 0, 2, 4, 6, 7)
    ph = ph.reshape(1, 1, hx, hy, hz, LEVELS - 1, blocks, 1, cheb)
    ph = jnp.broadcast_to(ph, ph.shape[:7] + (repeat, cheb))
    ph = ph.reshape(
        1, 1, hx, hy, hz, LEVELS - 1, count_x, blocks * repeat // count_x, cheb
    )
    ph = lax.all_to_all(ph, "gx", split_axis=6, concat_axis=0, tiled=True)
    ph = lax.all_to_all(ph, ("gy", "gz"), split_axis=7, concat_axis=1, tiled=True)
    ph = ph.reshape(count_x, count_y, count_z, hx, hy, hz, LEVELS - 1, block_share, cheb)
    ph = ph.transpose(6, 0, 3, 1, 4, 2, 5, 7, 8)
    ph = ph.reshape(LEVELS - 1, top, top, top, block_share, cheb)

    parts = [
        v.reshape(C, 2, count_x // 2, 2, count_y // 2, 2, count_z // 2, share, cheb)
        for v in first_rotate(weights, angles[0], (lx, ly, lz))
    ]
    where = {"gx": 1, "gy": 3, "gz": 5}
    orders = [("gx", "gy", "gz"), ("gy", "gz", "gx"), ("gz", "gx", "gy")]
    cuts = [C * i // 3 for i in range(4)]
    streams = {}
    for p in range(2):
        for k in range(3):
            if cuts[k + 1] > cuts[k]:
                streams[p, k] = parts[p][cuts[k] : cuts[k + 1]]
    for step in range(3):
        for p, k in list(streams):
            name = orders[k][step]
            streams[p, k] = halve_sum(streams[p, k], name, where[name])
    both = jnp.stack(
        [jnp.concatenate([streams[p, k] for k in range(3) if (p, k) in streams]) for p in range(2)]
    )
    both = both.reshape(2, C, count_x // 2, count_y // 2, count_z // 2, share, cheb)
    for dim, name in ((2, "gx"), (3, "gy"), (4, "gz")):
        both = exchange_low(both, name, dim)
    both = both.reshape(
        2, hx, hy, hz, count_x // 2, count_y // 2, count_z // 2, block_share, rhs_share, cheb
    )
    summed = both.transpose(0, 4, 1, 5, 2, 6, 3, 7, 8, 9)
    q = top // 2
    summed = summed.reshape(2, q * q * q * share, cheb)

    def translate(s):
        return jnp.einsum(
            "crk,tkn->ctrn", s, translation, preferred_element_type=jnp.float32
        ).astype(jnp.bfloat16)

    tail = (block_share, rhs_share, cheb)
    w = translate(summed)
    w = w.reshape((2, 2, 2, 2, 2, 2, 2, 2, 2, 2) + tail)
    ang = ph[0].reshape((2,) * 9 + (block_share, cheb))
    ang = ang.transpose(0, 3, 6, 1, 2, 4, 5, 7, 8, 9, 10)
    r, i = rotate_sum(w, ang)
    summed = jnp.stack([r.sum((3, 5, 7)), i.sum((3, 5, 7))]).astype(jnp.bfloat16)
    w = translate(summed.reshape(2, q * q * q * share, cheb))
    w = w.reshape((2,) + (2,) * 9 + tail)
    ang = ph[1].reshape((2,) * 9 + (block_share, cheb))
    ang = ang.transpose(1, 4, 7, 0, 3, 6, 2, 5, 8, 9, 10)
    r, i = rotate_sum(w, ang)
    summed = jnp.stack([r.sum((6, 7, 8)), i.sum((6, 7, 8))]).astype(jnp.bfloat16)
    summed = summed.transpose(4, 1, 5, 2, 6, 3, 0, 7, 8, 9)
    summed = summed.reshape(q, q, q, 2, share, cheb)
    keep = []
    for d, c in enumerate(counts):
        if c > q:
            summed = jnp.repeat(summed, c // q, axis=d)
        keep.append(max(1, q // c))
    kx, ky, kz = keep
    leaving = summed.reshape(count_x, kx, count_y, ky, count_z, kz, 2, share, cheb)
    leaving = leaving.transpose(0, 2, 4, 1, 3, 5, 6, 7, 8)
    leaving = leaving.reshape(count_x, count_yz, kx, ky, kz, 2, 1, share, cheb)
    back = lax.all_to_all(leaving, "gx", split_axis=0, concat_axis=6, tiled=True)
    back = lax.all_to_all(back, ("gy", "gz"), split_axis=1, concat_axis=7, tiled=True)
    back = back.reshape(kx, ky, kz, 2, lx, ly, lz, rhs, cheb)

    mats = translation.reshape(2, 2, 2, cheb, cheb)
    for d, (c, name) in enumerate(zip(counts, AXES)):
        if c > q:
            mats = lax.dynamic_index_in_dim(mats, lax.axis_index(name) % 2, d, keepdims=True)
    return last_translate(back, mats, weights.shape)


def last_kernel(e_ref, t_ref, o_ref):
    rows = e_ref[0, 0]
    lx, ly, kz, nz, m, cheb = (o_ref.shape[1],) + tuple(o_ref.shape[3:])
    for z in range(nz):
        r = jnp.dot(rows, t_ref[0, 0, z], preferred_element_type=jnp.float32)
        o_ref[0, :, 0, :, :, z] = r.astype(jnp.bfloat16).reshape(lx, ly, kz, m, cheb)


def last_translate(back, mats, out_shape):
    kx, ky, kz, _, lx, ly, lz, rhs, cheb = back.shape
    nx, ny, nz = mats.shape[:3]
    m = lz * 2 * rhs
    rows = back.transpose(0, 1, 4, 5, 2, 6, 3, 7, 8).reshape(kx, ky, lx * ly * kz * m, cheb)
    out = pl.pallas_call(
        last_kernel,
        grid=(nx, ny, kx, ky),
        in_specs=[
            pl.BlockSpec((1, 1, lx * ly * kz * m, cheb), lambda x, y, a, b: (a, b, 0, 0)),
            pl.BlockSpec((1, 1, nz, cheb, cheb), lambda x, y, a, b: (x, y, 0, 0, 0)),
        ],
        out_specs=pl.BlockSpec(
            (1, lx, 1, ly, kz, nz, m, cheb),
            lambda x, y, a, b: (a * nx + x, 0, b * ny + y, 0, 0, 0, 0, 0),
        ),
        out_shape=jax.ShapeDtypeStruct(
            (kx * nx, lx, ky * ny, ly, kz, nz, m, cheb), jnp.bfloat16
        ),
        compiler_params=pltpu.CompilerParams(vmem_limit_bytes=40 * 2**20),
        name="last_translate",
    )(rows, mats)
    return out.reshape(out_shape)


def first_kernel(w_ref, a_ref, re_ref, im_ref, cos_ref, sin_ref):
    ly, count_z = a_ref.shape[3], a_ref.shape[4]
    lz = re_ref.shape[5]
    cosine, sine = sincos(a_ref[0, 0, 0])
    cos_ref[...] = cosine
    sin_ref[...] = sine

    @pl.loop(0, ly)
    def _(l):
        for z in range(count_z):
            c = cos_ref[l, z : z + 1, :]
            s = sin_ref[l, z : z + 1, :]
            re = w_ref[0, 0, 0, l, z, 0].astype(jnp.float32)
            im = w_ref[0, 0, 0, l, z, 1].astype(jnp.float32)
            re_ref[0, 0, z // lz, 0, l, z % lz] = (re * c - im * s).astype(jnp.bfloat16)
            im_ref[0, 0, z // lz, 0, l, z % lz] = (re * s + im * c).astype(jnp.bfloat16)


def first_rotate(weights, angle, low):
    lx, ly, lz = low
    sx, sy, sz, _, rhs, cheb = weights.shape
    hx, hy, hz = sx // lx, sy // ly, sz // lz
    shape = (hx, hy, hz, lx, ly, lz, rhs, cheb)
    out = jax.ShapeDtypeStruct(shape, jnp.bfloat16)
    spec = pl.BlockSpec(
        (1, 1, hz, 1, ly, lz, rhs, cheb), lambda a, x, b: (a, b, 0, x, 0, 0, 0, 0)
    )
    return pl.pallas_call(
        first_kernel,
        grid=(hx, lx, hy),
        in_specs=[
            pl.BlockSpec(
                (1, 1, 1, ly, sz, 2, rhs, cheb), lambda a, x, b: (a, x, b, 0, 0, 0, 0, 0)
            ),
            pl.BlockSpec((1, 1, 1, ly, sz, cheb), lambda a, x, b: (a, x, b, 0, 0, 0)),
        ],
        out_specs=[spec, spec],
        out_shape=[out, out],
        scratch_shapes=[pltpu.VMEM((ly, sz, cheb), jnp.float32)] * 2,
        compiler_params=pltpu.CompilerParams(vmem_limit_bytes=40 * 2**20),
        name="first_rotate",
    )(
        weights.reshape(hx, lx, hy, ly, sz, 2, rhs, cheb),
        angle.reshape(hx, lx, hy, ly, sz, cheb),
    )


def solution(mesh):
    in_specs = (P("gx", "gy", "gz", None, None, None), P(None, "gx", "gy", "gz", None), P())
    out_specs = P("gx", "gy", "gz", None, None, None)
    return jax.shard_map(shards, mesh=mesh, in_specs=in_specs, out_specs=out_specs, check_vma=False)
```

profile of v0, /device:TPU:9, one launch (start us, length us, event | category | flops | bytes accessed | tf_op | source)
XLA Modules:
  0.0 542.2 jit_solution(8783615864773938586)
XLA Ops:
  1.8 24.4 %first_rotate.1 = (bf16[2,4,2,4,4,4,8,512]{7,6,5,4,3,2,1,0:T(8,128)(2,1)S(1)}, bf16[2,4,2,4,4,4,8,512]{7,6,5,4,3,2,1,0:T(8,128)(2,1)}) custom-call(bf16[2,4,4,4,8,2,8,512]{7,6,5,4,3,2,1,0:T(8,128)(2,1)} %bitcast.126, f32[2,4,4,4,8,512]{5,4,3,2,1,0:T(8,128)S(1)} %bitcast.109), custom_call_target="tpu_custom_call" | custom-call | tf_op jit(solution)/shard_map/first_rotate/pallas_call | solution.py:213
  36.9 4.8 constant_dynamic-slice_fusion.11
  77.7 5.2 all-to-all-start.2
  84.6 67.9 %collective-permute-done = bf16[5,1,2,2,1,2,2,16,512]{8,7,6,0,2,5,4,3,1:T(8,128)(2,1)} collective-permute-done((bf16[5,1,2,2,1,2,2,16,512]{8,7,6,0,2,5,4,3,1:T(8,128)(2,1)}, bf16[5,1,2,2,1,2,2,16,512]{8,7,6,0,2,5,4,3,1:T(8,128)(2,1)}, u32[]{:S(2)}, u32[]{:S(2)}) %collective-permute-start) | collective-permute-done | bytes 1310752 | tf_op jit(solution)/shard_map/ppermute | solution.py:31
  159.1 21.5 %collective-permute-done.9 = bf16[5,1,2,2,1,2,2,16,512]{8,7,6,0,2,5,4,3,1:T(8,128)(2,1)} collective-permute-done((bf16[5,1,2,2,1,2,2,16,512]{8,7,6,0,2,5,4,3,1:T(8,128)(2,1)}, bf16[5,1,2,2,1,2,2,16,512]{8,7,6,0,2,5,4,3,1:T(8,128)(2,1)}, u32[]{:S(2)}, u32[]{:S(2)}) %collective-permute-start.9) | collective-permute-done | bytes 1310752 | tf_op jit(solution)/shard_map/ppermute | solution.py:31
  194.3 7.7 %collective-permute-done.4 = bf16[5,2,2,1,1,1,2,16,512]{8,7,6,0,2,5,4,3,1:T(8,128)(2,1)S(1)} collective-permute-done((bf16[5,2,2,1,1,1,2,16,512]{8,7,6,0,2,5,4,3,1:T(8,128)(2,1)S(1)}, bf16[5,2,2,1,1,1,2,16,512]{8,7,6,0,2,5,4,3,1:T(8,128)(2,1)S(1)}, u32[]{:S(2)}, u32[]{:S(2)}) %collective-permute-start.4) | collective-permute-done | bytes 655392 | tf_op jit(solution)/shard_map/ppermute | solution.py:31
  207.0 9.0 %collective-permute-done.13 = bf16[5,2,2,1,1,1,2,16,512]{8,7,6,0,2,5,4,3,1:T(8,128)(2,1)S(1)} collective-permute-done((bf16[5,2,2,1,1,1,2,16,512]{8,7,6,0,2,5,4,3,1:T(8,128)(2,1)S(1)}, bf16[5,2,2,1,1,1,2,16,512]{8,7,6,0,2,5,4,3,1:T(8,128)(2,1)S(1)}, u32[]{:S(2)}, u32[]{:S(2)}) %collective-permute-start.13) | collective-permute-done | bytes 655392 | tf_op jit(solution)/shard_map/ppermute | solution.py:31
  217.5 5.5 %collective-permute-done.2 = bf16[5,1,2,1,1,1,2,16,512]{8,7,6,0,2,5,4,3,1:T(8,128)(2,1)S(1)} collective-permute-done((bf16[5,1,2,1,1,1,2,16,512]{8,7,6,0,2,5,4,3,1:T(8,128)(2,1)S(1)}, bf16[5,1,2,1,1,1,2,16,512]{8,7,6,0,2,5,4,3,1:T(8,128)(2,1)S(1)}, u32[]{:S(2)}, u32[]{:S(2)}) %collective-permute-start.2) | collective-permute-done | bytes 327712 | tf_op jit(solution)/shard_map/ppermute | solution.py:31
  226.2 65.2 %collective-permute-done.5 = bf16[5,1,2,1,1,1,2,16,512]{8,7,6,0,2,5,4,3,1:T(8,128)(2,1)S(1)} collective-permute-done((bf16[5,1,2,1,1,1,2,16,512]{8,7,6,0,2,5,4,3,1:T(8,128)(2,1)S(1)}, bf16[5,1,2,1,1,1,2,16,512]{8,7,6,0,2,5,4,3,1:T(8,128)(2,1)S(1)}, u32[]{:S(2)}, u32[]{:S(2)}) %collective-permute-start.5) | collective-permute-done | bytes 327712 | tf_op jit(solution)/shard_map/ppermute | solution.py:31
  302.5 8.2 %collective-permute-done.17 = bf16[6,1,2,1,1,1,2,16,512]{8,7,6,0,2,5,4,3,1:T(8,128)(2,1)S(1)} collective-permute-done((bf16[6,1,2,1,1,1,2,16,512]{8,7,6,0,2,5,4,3,1:T(8,128)(2,1)S(1)}, bf16[6,1,2,1,1,1,2,16,512]{8,7,6,0,2,5,4,3,1:T(8,128)(2,1)S(1)}, u32[]{:S(2)}, u32[]{:S(2)}) %collective-permute-start.17) | collective-permute-done | bytes 393248 | tf_op jit(solution)/shard_map/ppermute | solution.py:31
  312.4 4.8 all-to-all-start
  320.2 18.1 %all-to-all-done = bf16[2,16,2,1,2,16,512]{6,5,4,1,0,3,2:T(8,128)(2,1)} async-done(((bf16[2,16,2,1,2,16,512]{6,5,4,1,0,3,2:T(8,128)(2,1)}), bf16[2,16,2,1,2,16,512]{6,5,4,1,0,3,2:T(8,128)(2,1)}, u32[]{:S(2)}, u32[]{:S(2)}) %all-to-all-start) | async-done | bytes 2097184 | tf_op jit(solution)/shard_map/all_to_all | solution.py:41
  340.1 8.6 %all_to_all.76 = bf16[2,16,2,1,2,16,512]{6,5,2,1,0,3,4:T(8,128)(2,1)} all-to-all(bf16[2,16,2,1,2,16,512]{6,5,2,1,0,3,4:T(8,128)(2,1)S(1)} %copy.68), channel_id=1, replica_groups={{0,1},{2,3},{4,5},{6,7},{8,9},{10,11},{12,13},{14,15},{16,17},{18,19},{..., dimensions={4} | all-to-all | bytes 4194304 | tf_op jit(solution)/shard_map/all_to_all | solution.py:41
  355.8 11.8 %convert_bitcast_fusion.1 = bf16[2,8,1024,512]{3,2,1,0:T(8,128)(2,1)} fusion(bf16[2,1024,512,1]{2,1,3,0:T(8,128)(2,1)S(1)} %bitcast.141, bf16[8,512,512]{2,1,0:T(8,128)(2,1)S(1)} %copy-done.1), kind=kOutput, calls=%fused_computation.17 | convolution fusion | flops 8598323200 | bytes 23068672 | tf_op jit(solution)/shard_map/crk,tkn->ctrn/dot_general | solution.py:114
  367.6 11.4 %fusion.19 = (bf16[1,8,1024,512]{3,2,1,0:T(8,128)(2,1)}, bf16[1,8,1024,512]{3,2,1,0:T(8,128)(2,1)}) fusion(bf16[2,8,1024,512]{3,2,1,0:T(8,128)(2,1)} %convert_bitcast_fusion.1), kind=kLoop, calls=%fused_computation.90 | loop fusion | bytes 33554432 | tf_op jit(solution)/shard_map/slice | solution.py:51
  387.6 5.4 fusion.10
  393.1 13.4 %fusion.1 = (bf16[2,2,2,2,2,2,2,8,512]{8,7,6,5,4,3,2,1,0:T(8,128)(2,1)S(1)}, bf16[2,2,2,2,2,2,2,8,512]{8,7,6,5,4,3,2,1,0:T(8,128)(2,1)}) fusion(bf16[2,2,2,2,2,2,2,2,2,2,8,512]{11,10,9,8,7,6,5,4,3,2,1,0:T(8,128)(2,1)S(1)} %bitcast.119, bf16[2,2,2,2,2,2,2,2,2,2,8,512]{11,10,9,8,7,6,5,4,3,2,1,0:T(8,128)(2,1)S(1)} %bitcast.116, ...), kind=kLoop, calls=%fused_computation.9 | loop fusion | flops 48758784 | bytes 25165824 | tf_op jit(solution)/shard_map/reduce_sum | solution.py:124
  406.5 13.7 %convert_bitcast_fusion = bf16[2,8,1024,512]{3,2,1,0:T(8,128)(2,1)} fusion(bf16[8,512,512]{2,1,0:T(8,128)(2,1)S(1)} %copy-done.2, bf16[1,1024,512]{2,1,0:T(8,128)(2,1)} %bitcast.143, bf16[1,1024,512]{2,1,0:T(8,128)(2,1)S(1)} %bitcast.142), kind=kOutput, calls=%fused_computation.16 | convolution fusion | flops 8602517504 | bytes 23068672 | tf_op jit(solution)/shard_map/crk,tkn->ctrn/dot_general | solution.py:114
  420.2 6.6 %fusion.18 = (bf16[1,8,1024,512]{3,2,1,0:T(8,128)(2,1)S(1)}, bf16[1,8,1024,512]{3,2,1,0:T(8,128)(2,1)S(1)}) fusion(bf16[2,8,1024,512]{3,2,1,0:T(8,128)(2,1)} %convert_bitcast_fusion), kind=kLoop, calls=%fused_computation.89 | loop fusion | bytes 33554432 | tf_op jit(solution)/shard_map/slice | solution.py:51
  428.0 5.4 %fusion.11 = (f32[2,2,2,2,2,2,2,2,2,2,512]{10,9,8,7,2,6,5,1,4,3,0:T(2,128)S(1)}, f32[2,2,2,2,2,2,2,2,2,2,512]{10,9,8,7,2,6,5,1,4,3,0:T(2,128)}) fusion(f32[2,2,2,2,2,2,2,2,2,2,512]{10,9,8,7,6,5,4,3,2,1,0:T(2,128)S(1)} %bitcast.124), kind=kLoop, calls=%fused_computation.32 | loop fusion | flops 7864320 | bytes 6291456 | tf_op jit(solution)/shard_map/sub | solution.py:22
  433.4 12.4 %fusion.5 = (bf16[2,2,2,2,2,2,2,8,512]{8,7,6,5,4,3,2,1,0:T(8,128)(2,1)S(1)}, bf16[2,2,2,2,2,2,2,8,512]{8,7,6,5,4,3,2,1,0:T(8,128)(2,1)S(1)}) fusion(bf16[2,2,2,2,2,2,2,2,2,2,8,512]{11,10,9,8,7,6,5,4,3,2,1,0:T(8,128)(2,1)S(1)} %bitcast.121, bf16[2,2,2,2,2,2,2,2,2,2,8,512]{11,10,9,8,7,6,5,4,3,2,1,0:T(8,128)(2,1)S(1)} %bitcast.120, ...), kind=kLoop, calls=%fused_computation.13 | loop fusion | flops 48758784 | bytes 25165824 | tf_op jit(solution)/shard_map/reduce_sum | solution.py:130
  446.6 52.5 %all_to_all.77 = bf16[4,8,1,2,1,2,1,16,512]{8,7,5,3,1,6,4,2,0:T(8,128)(2,1)S(1)} all-to-all(bf16[4,8,1,2,1,2,1,16,512]{8,7,5,3,1,6,4,2,0:T(8,128)(2,1)S(1)} %bitcast.136), channel_id=1, replica_groups=mesh['gx'=4,'gy'=2,'gz'=4] {'gx'}, dimensions={0} | all-to-all | bytes 4194304 | tf_op jit(solution)/shard_map/all_to_all | solution.py:142
  499.4 30.3 %all_to_all.78 = bf16[1,8,1,2,1,2,4,16,512]{8,7,5,3,6,4,2,0,1:T(8,128)(2,1)S(1)} all-to-all(bf16[1,8,1,2,1,2,4,16,512]{8,7,5,3,6,4,2,0,1:T(8,128)(2,1)S(1)} %copy.85), channel_id=1, replica_groups=mesh['gx'=4,'gy'=2,'gz'=4] {'gy','gz'}, dimensions={1} | all-to-all | bytes 4194304 | tf_op jit(solution)/shard_map/all_to_all | solution.py:143
  530.2 11.6 %last_translate.1 = bf16[2,4,4,4,1,2,64,512]{7,6,5,4,3,2,1,0:T(8,128)(2,1)} custom-call(bf16[1,2,1024,512]{3,2,1,0:T(8,128)(2,1)S(1)} %bitcast.112, bf16[2,2,2,512,512]{4,3,2,1,0:T(8,128)(2,1)S(1)} %bitcast.113), custom_call_target="tpu_custom_call" | custom-call | tf_op jit(solution)/shard_map/last_translate/pallas_call | solution.py:166
  (132 shorter events, 115.8 us)
Async XLA Ops:
  42.9 109.7 %collective-permute-start = (bf16[5,1,2,2,1,2,2,16,512]{8,7,6,0,2,5,4,3,1:T(8,128)(2,1)}, bf16[5,1,2,2,1,2,2,16,512]{8,7,6,0,2,5,4,3,1:T(8,128)(2,1)}, u32[]{:S(2)}, u32[]{:S(2)}) collective-permute-start(bf16[5,1,2,2,1,2,2,16,512]{8,7,6,0,2,5,4,3,1:T(8,128)(2,1)} %copy.92), channel_id=1, source_target_pairs={{0,16},{8,24},{16,0},{24,8},{1,17},{9,25},{17,1},{25,9},{2,18},{10... | collective-permute-start | bytes 3932168 | tf_op jit(solution)/shard_map/ppermute | solution.py:31
  50.2 105.6 %collective-permute-start.3 = (bf16[5,2,2,1,1,2,2,16,512]{8,7,6,0,2,5,4,3,1:T(8,128)(2,1)}, bf16[5,2,2,1,1,2,2,16,512]{8,7,6,0,2,5,4,3,1:T(8,128)(2,1)}, u32[]{:S(2)}, u32[]{:S(2)}) collective-permute-start(bf16[5,2,2,1,1,2,2,16,512]{8,7,6,0,2,5,4,3,1:T(8,128)(2,1)} %copy.95), channel_id=1, source_target_pairs={{0,4},{4,0},{1,5},{5,1},{2,6},{6,2},{3,7},{7,3},{8,12},{12,8},{9,1... | collective-permute-start | bytes 3932168 | tf_op jit(solution)/shard_map/ppermute | solution.py:31
  52.7 128.0 %collective-permute-start.9 = (bf16[5,1,2,2,1,2,2,16,512]{8,7,6,0,2,5,4,3,1:T(8,128)(2,1)}, bf16[5,1,2,2,1,2,2,16,512]{8,7,6,0,2,5,4,3,1:T(8,128)(2,1)}, u32[]{:S(2)}, u32[]{:S(2)}) collective-permute-start(bf16[5,1,2,2,1,2,2,16,512]{8,7,6,0,2,5,4,3,1:T(8,128)(2,1)} %copy.101), channel_id=1, source_target_pairs={{0,16},{8,24},{16,0},{24,8},{1,17},{9,25},{17,1},{25,9},{2,18},{10... | collective-permute-start | bytes 3932168 | tf_op jit(solution)/shard_map/ppermute | solution.py:31
  64.7 122.5 %collective-permute-start.6 = (bf16[6,2,2,2,1,1,2,16,512]{8,7,6,0,2,5,4,3,1:T(8,128)(2,1)}, bf16[6,2,2,2,1,1,2,16,512]{8,7,6,0,2,5,4,3,1:T(8,128)(2,1)}, u32[]{:S(2)}, u32[]{:S(2)}) collective-permute-start(bf16[6,2,2,2,1,1,2,16,512]{8,7,6,0,2,5,4,3,1:T(8,128)(2,1)} %copy.98), channel_id=1, source_target_pairs={{0,2},{1,3},{2,0},{3,1},{4,6},{5,7},{6,4},{7,5},{8,10},{9,11},{10,... | collective-permute-start | bytes 4718600 | tf_op jit(solution)/shard_map/ppermute | solution.py:31
  66.0 117.9 %collective-permute-start.12 = (bf16[5,2,2,1,1,2,2,16,512]{8,7,6,0,2,5,4,3,1:T(8,128)(2,1)S(1)}, bf16[5,2,2,1,1,2,2,16,512]{8,7,6,0,2,5,4,3,1:T(8,128)(2,1)}, u32[]{:S(2)}, u32[]{:S(2)}) collective-permute-start(bf16[5,2,2,1,1,2,2,16,512]{8,7,6,0,2,5,4,3,1:T(8,128)(2,1)S(1)} %copy.104), channel_id=1, source_target_pairs={{0,4},{4,0},{1,5},{5,1},{2,6},{6,2},{3,7},{7,3},{8,12},{12,8},{9,1... | collective-permute-start | bytes 3932168 | tf_op jit(solution)/shard_map/ppermute | solution.py:31
  77.7 234.7 %all-to-all-start.2 = ((bf16[1,1,2,4,2,2,4,16,512]{8,7,5,4,3,2,1,0,6:T(8,128)(2,1)}), bf16[1,1,2,4,2,2,4,16,512]{8,7,5,4,3,2,1,0,6:T(8,128)(2,1)S(1)}, u32[]{:S(2)}, u32[]{:S(2)}) async-start(bf16[1,1,2,4,2,2,4,16,512]{8,7,5,4,3,2,1,0,6:T(8,128)(2,1)} %copy.71), calls=%async_computation.2 | async-start | bytes 4194304 | tf_op jit(solution)/shard_map/all_to_all | solution.py:78
  82.9 70.8 %copy-start.11 = (bf16[5,1,2,2,1,2,2,16,512]{8,7,6,5,3,2,1,0,4:T(8,128)(2,1)S(1)}, bf16[5,1,2,2,1,2,2,16,512]{8,7,6,5,3,2,1,0,4:T(8,128)(2,1)}, u32[]{:S(2)}) copy-start(bf16[5,1,2,2,1,2,2,16,512]{8,7,6,5,3,2,1,0,4:T(8,128)(2,1)} %get-tuple-element.42) | copy-start | bytes 3932164
  152.5 37.3 %collective-permute-start.15 = (bf16[6,2,2,2,1,1,2,16,512]{8,7,6,0,2,5,4,3,1:T(8,128)(2,1)S(1)}, bf16[6,2,2,2,1,1,2,16,512]{8,7,6,0,2,5,4,3,1:T(8,128)(2,1)S(1)}, u32[]{:S(2)}, u32[]{:S(2)}) collective-permute-start(bf16[6,2,2,2,1,1,2,16,512]{8,7,6,0,2,5,4,3,1:T(8,128)(2,1)S(1)} %copy.107), channel_id=1, source_target_pairs={{0,2},{1,3},{2,0},{3,1},{4,6},{5,7},{6,4},{7,5},{8,10},{9,11},{10,... | collective-permute-start | bytes 4718600 | tf_op jit(solution)/shard_map/ppermute | solution.py:31
  155.8 38.1 %collective-permute-start.1 = (bf16[5,1,2,1,1,2,2,16,512]{8,7,6,0,2,5,4,3,1:T(8,128)(2,1)S(1)}, bf16[5,1,2,1,1,2,2,16,512]{8,7,6,0,2,5,4,3,1:T(8,128)(2,1)S(1)}, u32[]{:S(2)}, u32[]{:S(2)}) collective-permute-start(bf16[5,1,2,1,1,2,2,16,512]{8,7,6,0,2,5,4,3,1:T(8,128)(2,1)S(1)} %constant_dynamic-slice_fusion.21), channel_id=1, source_target_pairs={{0,4},{4,0},{1,5},{5,1},{2,6},{6,2},{3,7},{7,3},{8,12},{12,8},{9,1... | collective-permute-start | bytes 1966088 | tf_op jit(solution)/shard_map/ppermute | solution.py:31
  157.1 24.8 %copy-start.9 = (bf16[5,1,2,2,1,2,2,16,512]{8,7,6,5,3,2,1,0,4:T(8,128)(2,1)S(1)}, bf16[5,1,2,2,1,2,2,16,512]{8,7,6,5,3,2,1,0,4:T(8,128)(2,1)}, u32[]{:S(2)}) copy-start(bf16[5,1,2,2,1,2,2,16,512]{8,7,6,5,3,2,1,0,4:T(8,128)(2,1)} %get-tuple-element.33) | copy-start | bytes 3932164
  180.6 21.3 %collective-permute-start.4 = (bf16[5,2,2,1,1,1,2,16,512]{8,7,6,0,2,5,4,3,1:T(8,128)(2,1)S(1)}, bf16[5,2,2,1,1,1,2,16,512]{8,7,6,0,2,5,4,3,1:T(8,128)(2,1)S(1)}, u32[]{:S(2)}, u32[]{:S(2)}) collective-permute-start(bf16[5,2,2,1,1,1,2,16,512]{8,7,6,0,2,5,4,3,1:T(8,128)(2,1)S(1)} %constant_dynamic-slice_fusion.17), channel_id=1, source_target_pairs={{0,2},{1,3},{2,0},{3,1},{4,6},{5,7},{6,4},{7,5},{8,10},{9,11},{10,... | collective-permute-start | bytes 1966088 | tf_op jit(solution)/shard_map/ppermute | solution.py:31
  183.9 19.6 %collective-permute-start.10 = (bf16[5,1,2,1,1,2,2,16,512]{8,7,6,0,2,5,4,3,1:T(8,128)(2,1)S(1)}, bf16[5,1,2,1,1,2,2,16,512]{8,7,6,0,2,5,4,3,1:T(8,128)(2,1)S(1)}, u32[]{:S(2)}, u32[]{:S(2)}) collective-permute-start(bf16[5,1,2,1,1,2,2,16,512]{8,7,6,0,2,5,4,3,1:T(8,128)(2,1)S(1)} %constant_dynamic-slice_fusion.9), channel_id=1, source_target_pairs={{0,4},{4,0},{1,5},{5,1},{2,6},{6,2},{3,7},{7,3},{8,12},{12,8},{9,1... | collective-permute-start | bytes 1966088 | tf_op jit(solution)/shard_map/ppermute | solution.py:31
  187.2 28.7 %collective-permute-start.13 = (bf16[5,2,2,1,1,1,2,16,512]{8,7,6,0,2,5,4,3,1:T(8,128)(2,1)S(1)}, bf16[5,2,2,1,1,1,2,16,512]{8,7,6,0,2,5,4,3,1:T(8,128)(2,1)S(1)}, u32[]{:S(2)}, u32[]{:S(2)}) collective-permute-start(bf16[5,2,2,1,1,1,2,16,512]{8,7,6,0,2,5,4,3,1:T(8,128)(2,1)S(1)} %constant_dynamic-slice_fusion.5), channel_id=1, source_target_pairs={{0,2},{1,3},{2,0},{3,1},{4,6},{5,7},{6,4},{7,5},{8,10},{9,11},{10,... | collective-permute-start | bytes 1966088 | tf_op jit(solution)/shard_map/ppermute | solution.py:31
  189.8 101.9 %collective-permute-start.7 = (bf16[6,1,2,2,1,1,2,16,512]{8,7,6,0,2,5,4,3,1:T(8,128)(2,1)S(1)}, bf16[6,1,2,2,1,1,2,16,512]{8,7,6,0,2,5,4,3,1:T(8,128)(2,1)S(1)}, u32[]{:S(2)}, u32[]{:S(2)}) collective-permute-start(bf16[6,1,2,2,1,1,2,16,512]{8,7,6,0,2,5,4,3,1:T(8,128)(2,1)S(1)} %constant_dynamic-slice_fusion.13), channel_id=1, source_target_pairs={{0,16},{8,24},{16,0},{24,8},{1,17},{9,25},{17,1},{25,9},{2,18},{10... | collective-permute-start | bytes 2359304 | tf_op jit(solution)/shard_map/ppermute | solution.py:31
  193.9 99.5 %collective-permute-start.16 = (bf16[6,1,2,2,1,1,2,16,512]{8,7,6,0,2,5,4,3,1:T(8,128)(2,1)S(1)}, bf16[6,1,2,2,1,1,2,16,512]{8,7,6,0,2,5,4,3,1:T(8,128)(2,1)S(1)}, u32[]{:S(2)}, u32[]{:S(2)}) collective-permute-start(bf16[6,1,2,2,1,1,2,16,512]{8,7,6,0,2,5,4,3,1:T(8,128)(2,1)S(1)} %constant_dynamic-slice_fusion.1), channel_id=1, source_target_pairs={{0,16},{8,24},{16,0},{24,8},{1,17},{9,25},{17,1},{25,9},{2,18},{10... | collective-permute-start | bytes 2359304 | tf_op jit(solution)/shard_map/ppermute | solution.py:31
  201.9 21.1 %collective-permute-start.2 = (bf16[5,1,2,1,1,1,2,16,512]{8,7,6,0,2,5,4,3,1:T(8,128)(2,1)S(1)}, bf16[5,1,2,1,1,1,2,16,512]{8,7,6,0,2,5,4,3,1:T(8,128)(2,1)S(1)}, u32[]{:S(2)}, u32[]{:S(2)}) collective-permute-start(bf16[5,1,2,1,1,1,2,16,512]{8,7,6,0,2,5,4,3,1:T(8,128)(2,1)S(1)} %constant_dynamic-slice_fusion.20), channel_id=1, source_target_pairs={{0,2},{1,3},{2,0},{3,1},{4,6},{5,7},{6,4},{7,5},{8,10},{9,11},{10,... | collective-permute-start | bytes 983048 | tf_op jit(solution)/shard_map/ppermute | solution.py:31
  203.5 88.0 %collective-permute-start.5 = (bf16[5,1,2,1,1,1,2,16,512]{8,7,6,0,2,5,4,3,1:T(8,128)(2,1)S(1)}, bf16[5,1,2,1,1,1,2,16,512]{8,7,6,0,2,5,4,3,1:T(8,128)(2,1)S(1)}, u32[]{:S(2)}, u32[]{:S(2)}) collective-permute-start(bf16[5,1,2,1,1,1,2,16,512]{8,7,6,0,2,5,4,3,1:T(8,128)(2,1)S(1)} %constant_dynamic-slice_fusion.16), channel_id=1, source_target_pairs={{0,16},{8,24},{16,0},{24,8},{1,17},{9,25},{17,1},{25,9},{2,18},{10... | collective-permute-start | bytes 983048 | tf_op jit(solution)/shard_map/ppermute | solution.py:31
  216.0 75.6 %collective-permute-start.11 = (bf16[5,1,2,1,1,1,2,16,512]{8,7,6,0,2,5,4,3,1:T(8,128)(2,1)S(1)}, bf16[5,1,2,1,1,1,2,16,512]{8,7,6,0,2,5,4,3,1:T(8,128)(2,1)S(1)}, u32[]{:S(2)}, u32[]{:S(2)}) collective-permute-start(bf16[5,1,2,1,1,1,2,16,512]{8,7,6,0,2,5,4,3,1:T(8,128)(2,1)S(1)} %constant_dynamic-slice_fusion.8), channel_id=1, source_target_pairs={{0,2},{1,3},{2,0},{3,1},{4,6},{5,7},{6,4},{7,5},{8,10},{9,11},{10,... | collective-permute-start | bytes 983048 | tf_op jit(solution)/shard_map/ppermute | solution.py:31
  223.0 75.5 %collective-permute-start.14 = (bf16[5,1,2,1,1,1,2,16,512]{8,7,6,0,2,5,4,3,1:T(8,128)(2,1)S(1)}, bf16[5,1,2,1,1,1,2,16,512]{8,7,6,0,2,5,4,3,1:T(8,128)(2,1)S(1)}, u32[]{:S(2)}, u32[]{:S(2)}) collective-permute-start(bf16[5,1,2,1,1,1,2,16,512]{8,7,6,0,2,5,4,3,1:T(8,128)(2,1)S(1)} %constant_dynamic-slice_fusion.4), channel_id=1, source_target_pairs={{0,16},{8,24},{16,0},{24,8},{1,17},{9,25},{17,1},{25,9},{2,18},{10... | collective-permute-start | bytes 983048 | tf_op jit(solution)/shard_map/ppermute | solution.py:31
  292.1 10.2 %collective-permute-start.8 = (bf16[6,1,2,1,1,1,2,16,512]{8,7,6,0,2,5,4,3,1:T(8,128)(2,1)S(1)}, bf16[6,1,2,1,1,1,2,16,512]{8,7,6,0,2,5,4,3,1:T(8,128)(2,1)S(1)}, u32[]{:S(2)}, u32[]{:S(2)}) collective-permute-start(bf16[6,1,2,1,1,1,2,16,512]{8,7,6,0,2,5,4,3,1:T(8,128)(2,1)S(1)} %constant_dynamic-slice_fusion.12), channel_id=1, source_target_pairs={{0,4},{4,0},{1,5},{5,1},{2,6},{6,2},{3,7},{7,3},{8,12},{12,8},{9,1... | collective-permute-start | bytes 1179656 | tf_op jit(solution)/shard_map/ppermute | solution.py:31
  293.7 17.0 %collective-permute-start.17 = (bf16[6,1,2,1,1,1,2,16,512]{8,7,6,0,2,5,4,3,1:T(8,128)(2,1)S(1)}, bf16[6,1,2,1,1,1,2,16,512]{8,7,6,0,2,5,4,3,1:T(8,128)(2,1)S(1)}, u32[]{:S(2)}, u32[]{:S(2)}) collective-permute-start(bf16[6,1,2,1,1,1,2,16,512]{8,7,6,0,2,5,4,3,1:T(8,128)(2,1)S(1)} %constant_dynamic-slice_fusion), channel_id=1, source_target_pairs={{0,4},{4,0},{1,5},{5,1},{2,6},{6,2},{3,7},{7,3},{8,12},{12,8},{9,1... | collective-permute-start | bytes 1179656 | tf_op jit(solution)/shard_map/ppermute | solution.py:31
  312.4 25.9 %all-to-all-start = ((bf16[2,16,2,1,2,16,512]{6,5,4,1,0,3,2:T(8,128)(2,1)}), bf16[2,16,2,1,2,16,512]{6,5,4,1,0,3,2:T(8,128)(2,1)}, u32[]{:S(2)}, u32[]{:S(2)}) async-start(bf16[2,16,2,1,2,16,512]{6,5,4,1,0,3,2:T(8,128)(2,1)} %maximum_bitcast_fusion), calls=%async_computation | async-start | bytes 4194304 | tf_op jit(solution)/shard_map/all_to_all | solution.py:41
  348.7 30.3 %all-to-all-start.3 = ((bf16[4,1,2,4,2,2,1,16,512]{8,0,5,4,3,2,6,1,7:T(4,128)(2,1)}), bf16[4,1,2,4,2,2,1,16,512]{8,0,5,4,3,2,6,1,7:T(4,128)(2,1)S(1)}, u32[]{:S(2)}, u32[]{:S(2)}) async-start(bf16[4,1,2,4,2,2,1,16,512]{8,0,5,4,3,2,6,1,7:T(4,128)(2,1)} %copy.72), calls=%async_computation.3 | async-start | bytes 4194304 | tf_op jit(solution)/shard_map/all_to_all | solution.py:79
  379.0 14.0 %slice-start.2 = ((s8[8388608]{0:T(1024)(128)(4,1)}), s8[4194304]{0:T(1024)(128)(4,1)S(1)}, s32[]{:S(2)}) async-start(s8[8388608]{0:T(1024)(128)(4,1)} %bitcast.117), calls=%async_computation.8 | async-start | bytes 8388608
  (14 other events, 80.0 us)
where the time goes:
time: 553 us; the launch traced here: 542 us
  waiting for transfers between devices  211 us (38%)
  blocking collectives  91.3 us (17%)
  local copies, waits for them, and re-layouts  84.2 us (15%)
  other arithmetic  54.2 us (10%)
  starting transfers between devices  38.7 us (7%)
  Pallas kernels  36 us (7%)
  matrix products  25.5 us (5%)
    ppermute x18, waiting for transfers between devices, halve_sum(): got = lax.ppermute(theirs, axis_name, pairs)  193 us
    all_to_all x1, blocking collectives, shards(): lax.all_to_all(leaving, 'gx', split_axis=0, concat_axis=6, tiled=True)  52.5 us
    all_to_all x1, blocking collectives, shards(): lax.all_to_all(back, ('gy', 'gz'), split_axis=1, concat_axis=7, tiled=True)  30.3 us
    dot_general x2, matrix products, translate(): jnp.einsum('crk,tkn->ctrn', s, translation, preferred_element_type=jnp.fl...  25.5 us
    pallas_call x1, Pallas kernels, first_rotate(): pl.pallas_call(first_kernel, grid=(hx, lx, hy), in_specs=[pl.BlockSpec((1...  24.4 us
    ppermute x18, starting transfers between devices, halve_sum(): got = lax.ppermute(theirs, axis_name, pairs)  24.4 us
    all_to_all x1, waiting for transfers between devices, exchange_low(): lax.all_to_all(terms, axis_name, split_axis=dim, concat_axis=dim, axis_in...  18.1 us
    slice x2, local copies, waits for them, and re-layouts, rotate_sum(): im = current[1].astype(jnp.float32)  18 us
  transfers between devices with their start and end apart: 21, of which 10 were waited for; matrix products, arithmetic and copies ran while one was open for 14% of the time, Pallas kernels for 0%

commit v1 on v0

--- a/solution.py
+++ b/solution.py
@@ -50,6 +50,503 @@
     re = current[0].astype(jnp.float32)
     im = current[1].astype(jnp.float32)
     return re * cosine - im * sine, re * sine + im * cosine
+
+
+MESH = pl.DeviceIdType.MESH
+
+
+def greet_all(counts):
+    ids = [lax.axis_index(a) for a in AXES]
+    total = counts[0] * counts[1] * counts[2]
+    barrier = pltpu.get_barrier_semaphore()
+
+    def other(r):
+        rel = (r // (counts[1] * counts[2]), r // counts[2] % counts[1], r % counts[2])
+        return tuple(lax.rem(i + d, c) for i, d, c in zip(ids, rel, counts))
+
+    def greet(r, carry):
+        pl.semaphore_signal(barrier, 1, device_id=other(r), device_id_type=MESH)
+        return carry
+
+    lax.fori_loop(1, total, greet, 0)
+    return ids, other, lambda: pl.semaphore_wait(barrier, total - 1)
+
+
+def remote(src, dst, send, recv, device):
+    return pltpu.make_async_remote_copy(
+        src, dst, send, recv, device_id=device, device_id_type=MESH
+    )
+
+
+def add(a, b):
+    return (a.astype(jnp.float32) + b.astype(jnp.float32)).astype(jnp.bfloat16)
+
+
+def exchange_kernel(
+    counts, w_ref, a_ref, b_ref, sum_ref, ph_ref,
+    w_win, a_win, cos_ref, sin_ref, term0, term1, got01, got02, got11, got12, half1, both, got3,
+    p_win, p_out, w_sem, a_sem, p_sem, own_sem, send_sem, got_sem, ph_send, ph_recv,
+):
+    cx, cy, cz = counts
+    sy, hy, _, _, _, hz = sum_ref.shape[:6]
+    lz = cz
+    sz = sy * hz * lz
+    lanes = a_ref.shape[-1] // 128
+    steps = sy * hy * hz
+    (gx, gy, gz), other, arrive = greet_all(counts)
+    me = (gx * cy + gy) * cz + gz
+
+    def loads(i):
+        s, h, z = i // (hy * hz), i // hz % hy, i % hz
+        slot = i % 2
+        out = []
+        for k in range(2):
+            out.append(
+                pltpu.make_async_copy(
+                    w_ref.at[k, :, h, :, s, pl.ds(z * lz, lz)], w_win.at[slot, k], w_sem.at[slot, k]
+                )
+            )
+            out.append(
+                pltpu.make_async_copy(a_ref.at[0, k, :, h, :, s], a_win.at[slot, k], a_sem.at[slot, k])
+            )
+        return out
+
+    def phase_load(u):
+        level, k = u // 2, u % 2
+
+        def start(n, carry):
+            h, lane = n // lanes, n % lanes
+            for c in range(cy):
+                pltpu.make_async_copy(
+                    b_ref.at[1 + level, k, :, h, c, :, pl.ds(pl.multiple_of(lane * 128, 128), 128)],
+                    p_win.at[u % 2, c, lane, :, pl.ds(pl.multiple_of(h * sz, sz), sz)],
+                    p_sem.at[u % 2],
+                ).start()
+            return carry
+
+        lax.fori_loop(0, hy * lanes, start, 0)
+
+    def rotate(i):
+        z = i % hz
+        slot = i % 2
+        for copy in loads(i):
+            copy.wait()
+
+        @pl.when(i + 1 < steps)
+        def _():
+            for copy in loads(i + 1):
+                copy.start()
+
+        def box(b, carry):
+            x, c = b // cy, b % cy
+            for k in range(2):
+                cosine, sine = sincos(a_win[slot, k, x, c])
+                cos_ref[k] = cosine
+                sin_ref[k] = sine
+            for k in range(2):
+                for r in range(lz):
+                    co = cos_ref[k, pl.ds(z * lz + r, 1), :]
+                    si = sin_ref[k, pl.ds(z * lz + r, 1), :]
+                    re = w_win[slot, k, x, c, r, 0].astype(jnp.float32)
+                    im = w_win[slot, k, x, c, r, 1].astype(jnp.float32)
+                    new_re = (re * co - im * si).astype(jnp.bfloat16)
+                    new_im = (re * si + im * co).astype(jnp.bfloat16)
+                    if k == 0:
+                        term0[i, c, r, x, 0] = new_re
+                        term0[i, c, r, x, 1] = new_im
+                    else:
+                        term1[i, r, c, x, 0] = new_re
+                        term1[i, r, c, x, 1] = new_im
+            return carry
+
+        lax.fori_loop(0, cx * cy, box, 0)
+
+    def along_y():
+        return (gx, 1 - gy, gz)
+
+    def along_z(r):
+        return (gx, gy, lax.rem(gz + r, cz))
+
+    def along_x(r):
+        return (lax.rem(gx + r, cx), gy, gz)
+
+    def first_send(i):
+        remote(term0.at[i, 1 - gy], got01.at[i], send_sem.at[0], got_sem.at[0, i], along_y()).start()
+        for r in range(1, cz):
+            to = along_z(r)
+            remote(
+                term1.at[i, to[2]], got11.at[i, cz - r - 1], send_sem.at[1], got_sem.at[1, i], to
+            ).start()
+
+    def second_send(i):
+        remote(half1.at[i, 1 - gy], got12.at[i], send_sem.at[3], got_sem.at[3, i], along_y()).start()
+        for r in range(1, cz):
+            to = along_z(r)
+            remote(
+                term0.at[i, gy, to[2]], got02.at[i, cz - r - 1], send_sem.at[2], got_sem.at[2, i], to
+            ).start()
+
+    def third_send(i):
+        for r in range(1, cx):
+            to = along_x(r)
+            remote(
+                both.at[i, to[0]], got3.at[i, cx - r - 1], send_sem.at[4], got_sem.at[4, i], to
+            ).start()
+
+    def first_sum(i):
+        remote(got01.at[i], got01.at[i], send_sem.at[0], got_sem.at[0, i], along_y()).wait_recv()
+        remote(got11.at[i], got11.at[i], send_sem.at[1], got_sem.at[1, i], along_z(1)).wait_recv()
+
+        def add0(b, carry):
+            term0[i, gy, b // cx, b % cx] = add(term0[i, gy, b // cx, b % cx], got01[i, b // cx, b % cx])
+            return carry
+
+        lax.fori_loop(0, lz * cx, add0, 0)
+
+        def add1(b, carry):
+            c, x = b // cx, b % cx
+            for j in range(cz // 2):
+                a = term1[i, gz, c, x] if j == 0 else got11[i, j - 1, c, x]
+                half1[i, c, x, lax.rem(gz + j, cz // 2)] = add(a, got11[i, j + cz // 2 - 1, c, x])
+            return carry
+
+        lax.fori_loop(0, cy * cx, add1, 0)
+
+    def second_sum(i):
+        remote(got02.at[i], got02.at[i], send_sem.at[2], got_sem.at[2, i], along_z(1)).wait_recv()
+        remote(got12.at[i], got12.at[i], send_sem.at[3], got_sem.at[3, i], along_y()).wait_recv()
+
+        def add2(x, carry):
+            for j in range(cz // 2):
+                a = term0[i, gy, gz, x] if j == 0 else got02[i, j - 1, x]
+                both[i, x, 0, lax.rem(gz + j, cz // 2)] = add(a, got02[i, j + cz // 2 - 1, x])
+            for j in range(cz // 2):
+                both[i, x, 1, j] = add(half1[i, gy, x, j], got12[i, x, j])
+            return carry
+
+        lax.fori_loop(0, cx, add2, 0)
+
+    def third_sum(i):
+        s, h, z = i // (hy * hz), i // hz % hy, i % hz
+        remote(got3.at[i], got3.at[i], send_sem.at[4], got_sem.at[4, i], along_x(1)).wait_recv()
+        for j in range(cx // 2):
+            for k in range(2):
+                for t in range(cz // 2):
+                    a = both[i, gx, k, t] if j == 0 else got3[i, j - 1, k, t]
+                    sum_ref[s, h, lax.rem(gx + j, cx // 2), k, t, z] = add(
+                        a, got3[i, j + cx // 2 - 1, k, t]
+                    )
+
+    def phases(u):
+        level, k = u // 2, u % 2
+        pltpu.make_async_copy(p_win.at[u % 2], p_win.at[u % 2], p_sem.at[u % 2]).wait()
+
+        rows = hy * sy * hz
+
+        def gather(b, carry):
+            c, x = b // cx, b % cx
+            for z in range(cz):
+                for lane in range(lanes):
+                    p_out[
+                        level, (x * cy + c) * cz + z, k, :, lane * 128 : (lane + 1) * 128
+                    ] = p_win[u % 2, c, lane, x, pl.ds(z, rows, stride=lz), :].astype(jnp.bfloat16)
+            return carry
+
+        lax.fori_loop(0, cx * cy, gather, 0)
+
+        @pl.when(u < 2)
+        def _():
+            phase_load(u + 2)
+
+        @pl.when(k == 1)
+        def _():
+            pltpu.make_async_copy(p_out.at[level, me], ph_ref.at[level, me], own_sem.at[level]).start()
+
+            def send(r, carry):
+                to = other(r)
+                at = (to[0] * cy + to[1]) * cz + to[2]
+                remote(
+                    p_out.at[level, at], ph_ref.at[level, me], ph_send.at[level], ph_recv.at[level], to
+                ).start()
+                return carry
+
+            lax.fori_loop(1, cx * cy * cz, send, 0)
+
+    for copy in loads(0):
+        copy.start()
+    for u in range(2):
+        phase_load(u)
+    rotate(0)
+    arrive()
+
+    def step(i, carry):
+        @pl.when(i < steps)
+        def _():
+            first_send(i)
+
+        @pl.when(i < 4)
+        def _():
+            phases(i)
+
+        @pl.when(i + 1 < steps)
+        def _():
+            rotate(i + 1)
+
+        @pl.when(jnp.logical_and(i >= 1, i < steps + 1))
+        def _():
+            first_sum(i - 1)
+            second_send(i - 1)
+
+        @pl.when(jnp.logical_and(i >= 2, i < steps + 2))
+        def _():
+            second_sum(i - 2)
+            third_send(i - 2)
+
+        @pl.when(i >= 3)
+        def _():
+            third_sum(i - 3)
+
+        return carry
+
+    lax.fori_loop(0, steps + 3, step, 0)
+    for level in range(2):
+        rest = pl.ds(0, cx * cy * cz - 1)
+        pltpu.make_async_copy(p_out.at[level, me], ph_ref.at[level, me], own_sem.at[level]).wait()
+        remote(
+            p_out.at[level, rest], ph_ref.at[level, rest], ph_send.at[level], ph_recv.at[level], other(1)
+        ).wait()
+    for n, ref in enumerate((got01, got11, got02, got12, got3)):
+        remote(ref, ref, send_sem.at[n], got_sem.at[n, 0], other(1)).wait_send()
+
+
+def exchange(weights, angles, counts, low):
+    cx, cy, cz = counts
+    X, Y, Z, _, R, K = weights.shape
+    hx, hy, hz, sy = X // low[0], Y // low[1], Z // low[2], low[1] // cy
+    steps = sy * hy * hz
+    total = cx * cy * cz
+    rows = hy * sy * hz
+    bf = jnp.bfloat16
+    unit = (2, R, K)
+
+    def vm(*shape):
+        return pltpu.VMEM(shape + unit, bf)
+
+    dma = pltpu.SemaphoreType.DMA
+    return pl.pallas_call(
+        lambda *refs: exchange_kernel(counts, *refs),
+        in_specs=[pl.BlockSpec(memory_space=pl.ANY)] * 3,
+        out_specs=[pl.BlockSpec(memory_space=pltpu.VMEM), pl.BlockSpec(memory_space=pl.ANY)],
+        out_shape=[
+            jax.ShapeDtypeStruct((sy, hy, cx // 2, hx, cz // 2, hz) + unit, bf),
+            jax.ShapeDtypeStruct((LEVELS - 1, total, hx, rows, K), bf),
+        ],
+        scratch_shapes=[
+            vm(2, 2, cx, cy, cz),
+            pltpu.VMEM((2, 2, cx, cy, Z, K), jnp.float32),
+            pltpu.VMEM((2, Z, K), jnp.float32),
+            pltpu.VMEM((2, Z, K), jnp.float32),
+            vm(steps, cy, cz, cx),
+            vm(steps, cz, cy, cx),
+            vm(steps, cz, cx),
+            vm(steps, cz - 1, cx),
+            vm(steps, cz - 1, cy, cx),
+            vm(steps, cx, cz // 2),
+            vm(steps, cy, cx, cz // 2),
+            vm(steps, cx, 2, cz // 2),
+            vm(steps, cx - 1, 2, cz // 2),
+            pltpu.VMEM((2, cy, K // 128, cx, hy * sy * Z, 128), jnp.float32),
+            pltpu.VMEM((LEVELS - 1, total, hx, rows, K), bf),
+            dma((2, 2)),
+            dma((2, 2)),
+            dma((2,)),
+            dma((LEVELS - 1,)),
+            dma((5,)),
+            dma((5, steps)),
+            dma((LEVELS - 1,)),
+            dma((LEVELS - 1,)),
+        ],
+        compiler_params=pltpu.CompilerParams(
+            collective_id=0, has_side_effects=True, vmem_limit_bytes=62 * 2**20
+        ),
+        name="exchange",
+    )(
+        weights.reshape(hx, cx, hy, cy, sy, Z, 2, R, K),
+        angles.reshape(LEVELS, hx, cx, hy, cy, sy, Z, K),
+        angles.reshape(LEVELS, hx, cx, hy, cy, sy * Z, K),
+    )
+
+
+def middle_kernel(
+    counts, s_ref, p_ref, t_ref, o_ref, cos_ref, sin_ref, buf0, buf1, mid_ref, st_ref,
+    own_sem, send_sem, got_sem,
+):
+    cx, cy, cz = counts
+    sy = s_ref.shape[0]
+    unit = s_ref.shape[3]
+    R = o_ref.shape[4]
+    total = cx * cy * cz
+    (gx, gy, gz), other, arrive = greet_all(counts)
+    me = (gx * cy + gy) * cz + gz
+    bufs = (buf0, buf1)
+
+    def turn(buf, base, level, q, row):
+        re = buf[base : base + R, :]
+        im = buf[base + R : base + 2 * R, :]
+        co = cos_ref[level, q, row : row + 1, :]
+        si = sin_ref[level, q, row : row + 1, :]
+        return re * co - im * si, re * si + im * co
+
+    def total_of(buf, terms):
+        acc = None
+        for term in terms:
+            new = turn(buf, *term)
+            acc = new if acc is None else (acc[0] + new[0], acc[1] + new[1])
+        return acc
+
+    def target(j):
+        dx, dy, dz = 1 - j // 4, 1 - j // 2 % 2, 1 - j % 2
+        return (
+            lax.rem(gx // 2 + dx, 2),
+            lax.rem(gy + dy, 2),
+            lax.rem(gz // 2 + dz, 2),
+        )
+
+    def owner(j, q):
+        tx, ty, tz = target(j)
+        return (tx * 2 + q // 2, ty, tz * 2 + q % 2)
+
+    def step(j, carry):
+        tx, ty, tz = target(j)
+        t4 = 4 * tx + 2 * ty + tz
+        for q in range(4):
+            to = owner(j, q)
+            at = (to[0] * cy + to[1]) * cz + to[2]
+            for level in range(LEVELS - 1):
+                for x in range(2):
+                    cosine, sine = sincos(p_ref[level, at, x].astype(jnp.float32))
+                    cos_ref[level, q * 2 + x] = cosine
+                    sin_ref[level, q * 2 + x] = sine
+
+        def first_dot(p):
+            s, y2 = p // 2, p % 2
+            for y3 in range(2):
+                bufs[p % 2][y3 * unit : (y3 + 1) * unit, :] = jnp.dot(
+                    s_ref[s, y3, y2], t_ref[t4], preferred_element_type=jnp.float32
+                )
+
+        def first_turn(p):
+            s, y2 = p // 2, p % 2
+            for x2 in range(2):
+                for z2 in range(2):
+                    terms = []
+                    for y3 in range(2):
+                        for x3 in range(2):
+                            for z3 in range(2):
+                                box = ((x3 * 2 + x2) * 2 + z3) * 2 + z2
+                                row = ((y3 * 2 + y2) * sy + s) * 2 + z2
+                                terms.append(
+                                    (y3 * unit + box * 2 * R, 0, (x3 * 2 + z3) * 2 + x2, row)
+                                )
+                    re, im = total_of(bufs[p % 2], terms)
+                    at = (((s * 2 + y2) * 2 + x2) * 2 + z2) * 2 * R
+                    mid_ref[at : at + R, :] = re.astype(jnp.bfloat16)
+                    mid_ref[at + R : at + 2 * R, :] = im.astype(jnp.bfloat16)
+
+        def second_dot(t):
+            bufs[t % 2][0 : mid_ref.shape[0], :] = jnp.dot(
+                mid_ref[...], t_ref[t], preferred_element_type=jnp.float32
+            )
+
+        def second_turn(t):
+            t3x, t3y, t3z = t // 4, t // 2 % 2, t % 2
+            q = t3x * 2 + t3z
+            for s in range(sy):
+                terms = []
+                for y2 in range(2):
+                    for x2 in range(2):
+                        for z2 in range(2):
+                            at = (((s * 2 + y2) * 2 + x2) * 2 + z2) * 2 * R
+                            row = ((t3y * 2 + y2) * sy + s) * 2 + z2
+                            terms.append((at, 1, q * 2 + x2, row))
+                re, im = total_of(bufs[t % 2], terms)
+                st_ref[j, q, t3y, s, 0] = re.astype(jnp.bfloat16)
+                st_ref[j, q, t3y, s, 1] = im.astype(jnp.bfloat16)
+
+        first_dot(0)
+        for p in range(2 * sy):
+            if p + 1 < 2 * sy:
+                first_dot(p + 1)
+            first_turn(p)
+        second_dot(0)
+        for t in range(8):
+            if t + 1 < 8:
+                second_dot(t + 1)
+            second_turn(t)
+
+        @pl.when(j == 0)
+        def _():
+            arrive()
+
+        for q in range(4):
+            to = owner(j, q)
+            at = (to[0] * cy + to[1]) * cz + to[2]
+
+            @pl.when(at == me)
+            def _():
+                pltpu.make_async_copy(st_ref.at[j, q], o_ref.at[me], own_sem).start()
+
+            @pl.when(at != me)
+            def _():
+                remote(st_ref.at[j, q], o_ref.at[me], send_sem, got_sem, to).start()
+
+        return carry
+
+    lax.fori_loop(0, 8, step, 0)
+    rest = o_ref.at[pl.ds(0, total - 1)]
+    pltpu.make_async_copy(o_ref.at[me], o_ref.at[me], own_sem).wait()
+    remote(rest, rest, send_sem, got_sem, other(1)).wait()
+
+
+def middle(summed, ph, translation, counts):
+    cx, cy, cz = counts
+    sy, hy, x3, hx, z3, hz, _, R, K = summed.shape
+    unit = x3 * hx * z3 * hz * 2 * R
+    total = cx * cy * cz
+    rows = hy * sy * hz
+    f32, bf = jnp.float32, jnp.bfloat16
+    dma = pltpu.SemaphoreType.DMA
+    return pl.pallas_call(
+        lambda *refs: middle_kernel(counts, *refs),
+        in_specs=[pl.BlockSpec(memory_space=pltpu.VMEM)] * 3,
+        out_specs=pl.BlockSpec(memory_space=pl.ANY),
+        out_shape=jax.ShapeDtypeStruct((total, 2, sy, 2, R, K), bf),
+        scratch_shapes=[
+            pltpu.VMEM((LEVELS - 1, 8, rows, K), f32),
+            pltpu.VMEM((LEVELS - 1, 8, rows, K), f32),
+            pltpu.VMEM((2 * unit, K), f32),
+            pltpu.VMEM((2 * unit, K), f32),
+            pltpu.VMEM((sy * 8 * 2 * R, K), bf),
+            pltpu.VMEM((8, 4, 2, sy, 2, R, K), bf),
+            dma,
+            dma,
+            dma,
+        ],
+        compiler_params=pltpu.CompilerParams(
+            collective_id=1, has_side_effects=True, vmem_limit_bytes=48 * 2**20
+        ),
+        name="middle",
+    )(summed.reshape(sy, 2, hy // 2, unit, K), ph, translation)
+
+
+def fast_shards(weights, angles, translation, counts, low):
+    cx, cy, cz = counts
+    summed, ph = exchange(weights, angles, counts, low)
+    final = middle(summed, ph, translation, counts)
+    sy, R, K = summed.shape[0], weights.shape[4], weights.shape[5]
+    back = final.reshape(cx, cy, cz, 2, sy, 2, R, K).transpose(3, 5, 0, 1, 4, 2, 6, 7)
+    back = back.reshape(1, 2, 1, 2, low[0], low[1], low[2], R, K)
+    return last_translate(back, translation.reshape(2, 2, 2, K, K), weights.shape)
 
 
 def shards(weights, angles, translation):
@@ -67,6 +564,8 @@
     rhs_share = share // block_share
     repeat = max(1, devices // blocks)
     C = hx * hy * hz
+    if (hx, hy, hz) == (2, 4, 2) and (lx, ly, lz) == (count_x, 2 * count_y, count_z):
+        return fast_shards(weights, angles, translation, counts, (lx, ly, lz))
 
     ph = angles[1:].astype(jnp.bfloat16)
     ph = ph.reshape(LEVELS - 1, hx, lx, hy, ly, hz, lz, cheb).transpose(1, 3, 5, 0, 2, 4, 6, 7)

time: 553 us -> 249 us (0.45); the launches traced: 542 us -> 249 us
  waiting for transfers between devices: 211 us -> 0 us
  Pallas kernels: 36 us -> 245 us
  blocking collectives: 91.3 us -> 0 us
  local copies, waits for them, and re-layouts: 84.2 us -> 3.76 us
  other arithmetic: 54.2 us -> 0 us
  starting transfers between devices: 38.7 us -> 0 us
  matrix products: 25.5 us -> 0 us
    pallas_call x1 -> x2, Pallas kernels: 24.4 us -> 234 us  [the longest x1 179 us: exchange(): pl.pallas_call(lambda *refs: exchange_kernel(counts, *refs), in_specs=[pl...]
    ppermute x18 -> x0, waiting for transfers between devices: 193 us -> none  [halve_sum(): got = lax.ppermute(theirs, axis_name, pairs)]
    all_to_all x3 -> x0, blocking collectives: 91.3 us -> none  [the longest x1 52.5 us: shards(): lax.all_to_all(leaving, 'gx', split_axis=0, concat_axis=6, tiled=True)]
    slice x8 -> x0, local copies, waits for them, and re-layouts: 35.6 us -> none  [the longest x2 18 us: rotate_sum(): im = current[1].astype(jnp.float32)]
    reduce_sum x2 -> x0, other arithmetic: 25.8 us -> none  [the longest x1 13.4 us: shards(): r.sum((3, 5, 7))]
    dot_general x2 -> x0, matrix products: 25.5 us -> none  [translate(): jnp.einsum('crk,tkn->ctrn', s, translation, preferred_element_type=jnp.fl...]
    ppermute x18 -> x0, starting transfers between devices: 24.4 us -> none  [halve_sum(): got = lax.ppermute(theirs, axis_name, pairs)]
    all_to_all x3 -> x0, waiting for transfers between devices: 18.1 us -> none  [the longest x1 18.1 us: exchange_low(): lax.all_to_all(terms, axis_name, split_axis=dim, concat_axis=dim, axis_in...]
  transfers between devices with their start and end apart: 21 -> 0, of which waited for: 10 -> 0; matrix products, arithmetic and copies ran while one was open for 14% -> 0% of each run, Pallas kernels for 0% -> 0%
where the time goes in v1:
time: 249 us
  Pallas kernels  245 us (98%)
  local copies, waits for them, and re-layouts  3.76 us (2%)
    pallas_call x1, Pallas kernels, exchange(): pl.pallas_call(lambda *refs: exchange_kernel(counts, *refs), in_specs=[pl...  179 us
    pallas_call x1, Pallas kernels, middle(): pl.pallas_call(lambda *refs: middle_kernel(counts, *refs), in_specs=[pl.B...  54.2 us
    pallas_call x1, Pallas kernels, last_translate(): pl.pallas_call(last_kernel, grid=(nx, ny, kx, ky), in_specs=[pl.BlockSpec...  11.5 us

profile of v1, /device:TPU:9, one launch (start us, length us, event | category | flops | bytes accessed | tf_op | source)
XLA Modules:
  0.0 249.0 jit_solution(14076697006638437236)
XLA Ops:
  0.0 179.4 %exchange.1 = (bf16[2,4,2,2,2,2,2,8,512]{8,7,6,5,4,3,2,1,0:T(8,128)(2,1)}, bf16[2,32,2,16,512]{4,3,2,1,0:T(8,128)(2,1)}) custom-call(bf16[2,4,4,2,2,8,2,8,512]{8,7,6,5,4,3,2,1,0:T(8,128)(2,1)} %bitcast.20, f32[3,2,4,4,2,2,8,512]{7,6,5,4,3,2,1,0:T(8,128)} %bitcast.18, f32[3,2,4,4,2,16,512]{6,5,4,3,2,1,0:T(8,128)} %bitcast.19), custom_call_target="tpu_custom_call" | custom-call | tf_op jit(solution)/shard_map/exchange/pallas_call | solution.py:336
  179.5 0.0 copy-start.1
  179.5 1.6 copy-done.1
  181.1 54.2 %middle.1 = bf16[32,2,2,2,8,512]{5,4,3,2,1,0:T(8,128)(2,1)S(1)} custom-call(bf16[2,2,2,256,512]{4,3,2,1,0:T(8,128)(2,1)S(1)} %bitcast.17, bf16[2,32,2,16,512]{4,3,2,1,0:T(8,128)(2,1)} %get-tuple-element.8.refs_1_, bf16[8,512,512]{2,1,0:T(8,128)(2,1)} %refs_2_.1), custom_call_target="tpu_custom_call" | custom-call | tf_op jit(solution)/shard_map/middle/pallas_call | solution.py:519
  235.2 0.0 copy-start
  235.2 0.2 copy.4
  235.5 1.9 copy-done
  237.4 11.5 %last_translate.1 = bf16[2,4,4,4,1,2,64,512]{7,6,5,4,3,2,1,0:T(8,128)(2,1)} custom-call(bf16[1,2,1024,512]{3,2,1,0:T(8,128)(2,1)S(1)} %bitcast.16, bf16[2,2,2,512,512]{4,3,2,1,0:T(8,128)(2,1)S(1)} %bitcast.14), custom_call_target="tpu_custom_call" | custom-call | tf_op jit(solution)/shard_map/last_translate/pallas_call | solution.py:665
Async XLA Ops:
  179.5 1.6 copy-start.1
  235.2 2.2 copy-start
